TPU v7x, 512 devices: a whole 4x4x16 slice. The times are simulated.
512 devices in a mesh: dp: 16 (over z), seq: 32 (over x, y, core).
Axes of the slice: x: 4, y: 4, z: 16, core: 2. Of those that a mesh axis runs over, the one named last changes fastest.
Arguments:
- query_rows: bfloat16 [65536, 4096], P(('dp', 'seq')), may hold values from -10 to 10
- source_key_rows: bfloat16 [65536, 1024], P(('dp', 'seq')), may hold values from -10 to 10
- source_value_rows: bfloat16 [65536, 1024], P(('dp', 'seq')), may hold values from -6 to 6
- grad_rows: bfloat16 [65536, 4096], P(('dp', 'seq')), may hold values from -6 to 6
- routes: int32 [65536, 1], P(('dp', 'seq')), may hold values from 0 to 15; in each aligned block of 128 rows (0 to 127, 128 to 255, ...) at most 8 rows name the same one
- segments: int32 [16, 4096], P('dp', 'seq'), may hold values from 0 to 15, never falling along the last dimension, each value on 1 to 512 neighbouring positions
Outputs:
- grad_query: bfloat16 [65536, 4096], P(('dp', 'seq'))
- packed_key_gradient: bfloat16 [65536, 1024], P(('dp', 'seq'))
- packed_value_gradient: bfloat16 [65536, 1024], P(('dp', 'seq'))
Inputs may be any that keep to these rules, and one draw needn't show every extreme that they name: `routes`: each pack number is named by exactly 8 of the rows of one device. `segments`: along a pack the document numbers never fall; a document covers 1 to 512 consecutive positions, and some document exactly 512.
All inputs are finite; a program needn't handle non-finite values.
Results may differ from a plain program's by a relative error of at most 0.012.
The roundings to bfloat16 on the way count: a program that leaves them out, or rounds other values in their place, can miss the bound.
Values may be sent and summed in bfloat16 or wider, within the bound.
A program may use at most 64 MiB of HBM per device.

v0:
```python
import jax
import jax.numpy as jnp
from jax import lax
from jax.sharding import PartitionSpec as P

QUERY_HEADS = 32
KEY_VALUE_HEADS = 8
HEAD_DIMENSION = 128
MAXDOC = 512


def place_rows(targets, n_groups):
    onehot = (targets[:, None] == jnp.arange(n_groups, dtype=jnp.int32)[None, :]).astype(jnp.int32)
    before = jnp.cumsum(onehot, axis=0) - onehot
    return jnp.sum(before * onehot, axis=1)


def widen_heads(key_value_rows):
    row_count = key_value_rows.shape[0]
    reshaped_array = key_value_rows.reshape(row_count, KEY_VALUE_HEADS, 1, HEAD_DIMENSION)
    return jnp.broadcast_to(
        reshaped_array, (row_count, KEY_VALUE_HEADS, QUERY_HEADS // KEY_VALUE_HEADS, HEAD_DIMENSION)
    ).reshape(row_count, QUERY_HEADS * HEAD_DIMENSION)


def attend(query_block, key_band, value_band, grad_block, seg_query, seg_keys, offset):
    score_scale = HEAD_DIMENSION ** (-0.5)
    scores = (
        jnp.einsum("ahd,jhd->haj", query_block, key_band, preferred_element_type=jnp.float32)
        * score_scale
    )
    row_pos = jnp.arange(query_block.shape[0], dtype=jnp.int32)[:, None]
    col_pos = jnp.arange(key_band.shape[0], dtype=jnp.int32)[None, :]
    allowed = (col_pos <= row_pos + offset) & (seg_keys[None, :] == seg_query[:, None])
    scores = jnp.where(allowed[None], scores, -jnp.inf)
    top_score = jnp.max(scores, axis=2, keepdims=True)
    weights = jnp.exp(scores - top_score)
    soft_prob = weights / jnp.sum(weights, axis=2, keepdims=True)
    prob_low = soft_prob.astype(jnp.bfloat16)
    output = jnp.einsum("haj,jhd->ahd", prob_low, value_band, preferred_element_type=jnp.float32)
    row_delta = jnp.sum(grad_block.astype(jnp.float32) * output, axis=2)
    grad_prob = jnp.einsum(
        "ahd,jhd->haj", grad_block, value_band, preferred_element_type=jnp.float32
    )
    grad_score = (soft_prob * (grad_prob - row_delta.T[:, :, None]) * score_scale).astype(
        jnp.bfloat16
    )
    grad_query = jnp.einsum(
        "haj,jhd->ahd", grad_score, key_band, preferred_element_type=jnp.float32
    ).astype(jnp.bfloat16)
    packed_key_gradient = jnp.einsum(
        "haj,ahd->jhd", grad_score, query_block, preferred_element_type=jnp.float32
    )
    packed_value_gradient = jnp.einsum(
        "haj,ahd->jhd", prob_low, grad_block, preferred_element_type=jnp.float32
    )
    return (grad_query, packed_key_gradient, packed_value_gradient)


def band_pass(head_q, head_k, head_v, head_g, seg_all, n_heads):
    total_rows = head_q.shape[0]
    block_width = MAXDOC
    blocks = total_rows // block_width

    def blocked(matrix):
        return matrix.reshape(blocks, block_width, n_heads, HEAD_DIMENSION)

    query_blocks = blocked(head_q)
    key_blocks = blocked(head_k)
    value_blocks = blocked(head_v)
    grad_blocks = blocked(head_g)
    key_prior = jnp.concatenate([jnp.zeros_like(key_blocks[:1]), key_blocks[:-1]], axis=0)
    value_prior = jnp.concatenate([jnp.zeros_like(value_blocks[:1]), value_blocks[:-1]], axis=0)
    seg_blocks = seg_all.reshape(blocks, block_width)
    seg_prior = jnp.concatenate(
        [jnp.full((1, block_width), -1, jnp.int32), seg_blocks[:-1]], axis=0
    )

    def block_step(scan_carry, inputs):
        (
            query_block,
            key_before,
            key_own,
            value_before,
            value_own,
            grad_block,
            seg_before,
            seg_own,
        ) = inputs
        result = attend(
            query_block,
            jnp.concatenate([key_before, key_own], 0),
            jnp.concatenate([value_before, value_own], 0),
            grad_block,
            seg_own,
            jnp.concatenate([seg_before, seg_own], 0),
            block_width,
        )
        return (scan_carry, result)

    unused, (grad_q, band_k, band_v) = lax.scan(
        block_step,
        jnp.int32(0),
        (
            query_blocks,
            key_prior,
            key_blocks,
            value_prior,
            value_blocks,
            grad_blocks,
            seg_prior,
            seg_blocks,
        ),
    )

    def fold_band(band_sum):
        own_part = band_sum[:, block_width:]
        later_part = jnp.concatenate(
            [band_sum[1:, :block_width], jnp.zeros_like(band_sum[:1, :block_width])], axis=0
        )
        return (
            (own_part + later_part)
            .astype(jnp.bfloat16)
            .reshape(total_rows, n_heads * HEAD_DIMENSION)
        )

    return (
        grad_q.reshape(total_rows, n_heads * HEAD_DIMENSION),
        fold_band(band_k),
        fold_band(band_v),
    )


def body(query_rows, source_key_rows, source_value_rows, grad_rows, routes, segments):
    n_dp = lax.axis_size("dp")
    n_seq = lax.axis_size("seq")
    resident_rows = query_rows.shape[0]
    capacity = resident_rows // n_dp
    n_heads = QUERY_HEADS // n_seq
    targets = routes[:, 0]
    slot_index = targets * capacity + place_rows(targets, n_dp)
    row_order = jnp.argsort(slot_index)
    moved_q, moved_k, moved_v = (
        lax.all_to_all(query_rows[row_order], "dp", split_axis=0, concat_axis=0, tiled=True),
        lax.all_to_all(source_key_rows[row_order], "dp", split_axis=0, concat_axis=0, tiled=True),
        lax.all_to_all(source_value_rows[row_order], "dp", split_axis=0, concat_axis=0, tiled=True),
    )
    head_q, head_k, head_v, head_g = (
        lax.all_to_all(moved_q, "seq", split_axis=1, concat_axis=0, tiled=True),
        lax.all_to_all(widen_heads(moved_k), "seq", split_axis=1, concat_axis=0, tiled=True),
        lax.all_to_all(widen_heads(moved_v), "seq", split_axis=1, concat_axis=0, tiled=True),
        lax.all_to_all(grad_rows, "seq", split_axis=1, concat_axis=0, tiled=True),
    )
    seg_all = lax.all_gather(segments, "seq", axis=1, tiled=True)[0]
    grad_q, grad_k, grad_v = band_pass(head_q, head_k, head_v, head_g, seg_all, n_heads)
    back_q, returned_key, returned_value = (
        lax.all_to_all(grad_q, "seq", split_axis=0, concat_axis=1, tiled=True),
        lax.all_to_all(grad_k, "seq", split_axis=0, concat_axis=1, tiled=True),
        lax.all_to_all(grad_v, "seq", split_axis=0, concat_axis=1, tiled=True),
    )
    group_member_count = QUERY_HEADS // KEY_VALUE_HEADS
    packed_key_gradient = (
        jnp.sum(
            returned_key.reshape(
                resident_rows, KEY_VALUE_HEADS, group_member_count, HEAD_DIMENSION
            ),
            axis=2,
            dtype=jnp.float32,
        )
        .astype(jnp.bfloat16)
        .reshape(resident_rows, KEY_VALUE_HEADS * HEAD_DIMENSION)
    )
    packed_value_gradient = (
        jnp.sum(
            returned_value.reshape(
                resident_rows, KEY_VALUE_HEADS, group_member_count, HEAD_DIMENSION
            ),
            axis=2,
            dtype=jnp.float32,
        )
        .astype(jnp.bfloat16)
        .reshape(resident_rows, KEY_VALUE_HEADS * HEAD_DIMENSION)
    )
    return (back_q, packed_key_gradient, packed_value_gradient)


def solution(mesh):
    placed = (
        P(("dp", "seq"), None),
        P(("dp", "seq"), None),
        P(("dp", "seq"), None),
        P(("dp", "seq"), None),
        P(("dp", "seq"), None),
        P("dp", "seq"),
    )
    return jax.shard_map(
        body,
        mesh=mesh,
        in_specs=placed,
        out_specs=(P(("dp", "seq"), None), P(("dp", "seq"), None), P(("dp", "seq"), None)),
        check_vma=False,
    )
```

profile of v0, /device:TPU:1, one launch (start us, length us, event | category | flops | bytes accessed | tf_op | source)
XLA Modules:
  0.0 393.5 jit_solution(10561196768373759649)
XLA Ops:
  3.2 2.5 sort.17
  5.7 2.7 gather_fusion.2
  8.5 15.9 %all-to-all-start.5 = ((bf16[16,8,1024]{2,1,0:T(8,128)(2,1)}), bf16[16,8,1024]{2,1,0:T(8,128)(2,1)S(1)}, u32[]{:S(2)}, u32[]{:S(2)}) async-start(bf16[16,8,1024]{2,1,0:T(8,128)(2,1)} %bitcast.37), calls=%async_computation.5 | async-start | bytes 524288 | tf_op jit(solution)/shard_map/all_to_all | solution.py:146
  25.9 11.6 %all-to-all-done.5 = bf16[16,8,1024]{2,1,0:T(8,128)(2,1)S(1)} async-done(((bf16[16,8,1024]{2,1,0:T(8,128)(2,1)}), bf16[16,8,1024]{2,1,0:T(8,128)(2,1)S(1)}, u32[]{:S(2)}, u32[]{:S(2)}) %all-to-all-start.5) | async-done | bytes 262176 | tf_op jit(solution)/shard_map/all_to_all | solution.py:146
  37.5 10.9 %all-to-all-start = ((bf16[16,8,1024]{2,1,0:T(8,128)(2,1)}), bf16[16,8,1024]{2,1,0:T(8,128)(2,1)S(1)}, u32[]{:S(2)}, u32[]{:S(2)}) async-start(bf16[16,8,1024]{2,1,0:T(8,128)(2,1)} %bitcast.23), calls=%async_computation | async-start | bytes 524288 | tf_op jit(solution)/shard_map/all_to_all | solution.py:145
  49.7 11.7 %all-to-all-done = bf16[16,8,1024]{2,1,0:T(8,128)(2,1)S(1)} async-done(((bf16[16,8,1024]{2,1,0:T(8,128)(2,1)}), bf16[16,8,1024]{2,1,0:T(8,128)(2,1)S(1)}, u32[]{:S(2)}, u32[]{:S(2)}) %all-to-all-start) | async-done | bytes 262176 | tf_op jit(solution)/shard_map/all_to_all | solution.py:145
  61.5 13.4 %all-to-all-start.4 = ((bf16[128,32,128]{0,2,1:T(8,128)(2,1)}), bf16[128,32,128]{0,2,1:T(8,128)(2,1)S(1)}, u32[]{:S(2)}, u32[]{:S(2)}) async-start(bf16[128,32,128]{0,2,1:T(8,128)(2,1)} %bitcast.34), calls=%async_computation.4 | async-start | bytes 2097152 | tf_op jit(solution)/shard_map/all_to_all | solution.py:152
  75.0 16.8 %all-to-all-done.4 = bf16[128,32,128]{0,2,1:T(8,128)(2,1)S(1)} async-done(((bf16[128,32,128]{0,2,1:T(8,128)(2,1)}), bf16[128,32,128]{0,2,1:T(8,128)(2,1)S(1)}, u32[]{:S(2)}, u32[]{:S(2)}) %all-to-all-start.4) | async-done | bytes 1048608 | tf_op jit(solution)/shard_map/all_to_all | solution.py:152
  93.1 4.5 %all-to-all-start.1 = ((bf16[128,32,128]{2,0,1:T(8,128)(2,1)}), bf16[128,32,128]{2,0,1:T(8,128)(2,1)}, u32[]{:S(2)}, u32[]{:S(2)}) async-start(bf16[128,32,128]{2,0,1:T(8,128)(2,1)} %bitcast.24), calls=%async_computation.1 | async-start | bytes 2097152 | tf_op jit(solution)/shard_map/all_to_all | solution.py:150
  97.6 2.2 gather_fusion.1
  99.7 14.8 %all-to-all-done.1 = bf16[128,32,128]{2,0,1:T(8,128)(2,1)} async-done(((bf16[128,32,128]{2,0,1:T(8,128)(2,1)}), bf16[128,32,128]{2,0,1:T(8,128)(2,1)}, u32[]{:S(2)}, u32[]{:S(2)}) %all-to-all-start.1) | async-done | bytes 1048608 | tf_op jit(solution)/shard_map/all_to_all | solution.py:150
  114.5 5.4 %all-to-all-start.2 = ((bf16[16,8,4096]{2,1,0:T(8,128)(2,1)}), bf16[16,8,4096]{2,1,0:T(8,128)(2,1)S(1)}, u32[]{:S(2)}, u32[]{:S(2)}) async-start(bf16[16,8,4096]{2,1,0:T(8,128)(2,1)} %bitcast.30), calls=%async_computation.2 | async-start | bytes 2097152 | tf_op jit(solution)/shard_map/all_to_all | solution.py:144
  120.0 46.3 %all-to-all-done.2 = bf16[16,8,4096]{2,1,0:T(8,128)(2,1)S(1)} async-done(((bf16[16,8,4096]{2,1,0:T(8,128)(2,1)}), bf16[16,8,4096]{2,1,0:T(8,128)(2,1)S(1)}, u32[]{:S(2)}, u32[]{:S(2)}) %all-to-all-start.2) | async-done | bytes 1048608 | tf_op jit(solution)/shard_map/all_to_all | solution.py:144
  167.6 8.7 %all-to-all-start.6 = ((bf16[128,32,128]{2,0,1:T(8,128)(2,1)}), bf16[128,32,128]{2,0,1:T(8,128)(2,1)}, u32[]{:S(2)}, u32[]{:S(2)}) async-start(bf16[128,32,128]{2,0,1:T(8,128)(2,1)} %bitcast.38), calls=%async_computation.6 | async-start | bytes 2097152 | tf_op jit(solution)/shard_map/all_to_all | solution.py:151
  178.0 15.4 %all-to-all-done.6 = bf16[128,32,128]{2,0,1:T(8,128)(2,1)} async-done(((bf16[128,32,128]{2,0,1:T(8,128)(2,1)}), bf16[128,32,128]{2,0,1:T(8,128)(2,1)}, u32[]{:S(2)}, u32[]{:S(2)}) %all-to-all-start.6) | async-done | bytes 1048608 | tf_op jit(solution)/shard_map/all_to_all | solution.py:151
  193.3 4.4 %all-to-all-start.3 = ((bf16[128,32,128]{2,0,1:T(8,128)(2,1)}), bf16[128,32,128]{2,0,1:T(8,128)(2,1)}, u32[]{:S(2)}, u32[]{:S(2)}) async-start(bf16[128,32,128]{2,0,1:T(8,128)(2,1)} %copy.62), calls=%async_computation.3 | async-start | bytes 2097152 | tf_op jit(solution)/shard_map/all_to_all | solution.py:149
  197.8 29.8 %all_gather.3 = s32[1,4096]{1,0:T(1,128)S(1)} all-gather(s32[1,128]{1,0:T(1,128)S(1)} %copy-done.4), channel_id=1, replica_groups=mesh['dp'=16,'seq'=32] {'seq'}, dimensions={1}, use_global_device_ids=true | all-gather | bytes 16896 | tf_op jit(solution)/shard_map/all_gather | solution.py:154
  234.9 93.0 %while.14 = (s32[]{:T(128)}, bf16[8,512,1,128]{3,1,0,2:T(8,128)(2,1)}, f32[8,1024,1,128]{3,1,0,2:T(8,128)}, f32[8,1024,1,128]{3,1,0,2:T(8,128)}, bf16[8,512,1,12...) while((s32[]{:T(128)}, ...), condition=%wide.region_7.8_spmd, body=%wide.region_3.7_spmd.sunk | while | flops 816054272 | bytes 27041960 | solution.py:101
  249.5 1.6 fusion.43
  261.2 1.6 fusion.43
  272.8 1.6 fusion.43
  319.3 1.6 fusion.43
  327.8 4.9 %all-to-all-start.7 = ((bf16[32,128,128]{2,1,0:T(8,128)(2,1)}), bf16[32,128,128]{2,1,0:T(8,128)(2,1)S(1)}, u32[]{:S(2)}, u32[]{:S(2)}) async-start(bf16[32,128,128]{2,1,0:T(8,128)(2,1)} %bitcast.165), calls=%async_computation.7 | async-start | bytes 2097152 | tf_op jit(solution)/shard_map/all_to_all | solution.py:157
  334.3 2.9 add_convert_fusion
  337.3 12.4 %all-to-all-done.7 = bf16[32,128,128]{2,1,0:T(8,128)(2,1)S(1)} async-done(((bf16[32,128,128]{2,1,0:T(8,128)(2,1)}), bf16[32,128,128]{2,1,0:T(8,128)(2,1)S(1)}, u32[]{:S(2)}, u32[]{:S(2)}) %all-to-all-start.7) | async-done | bytes 1048608 | tf_op jit(solution)/shard_map/all_to_all | solution.py:157
  350.6 4.0 %all-to-all-start.9 = ((bf16[32,128,128]{2,1,0:T(8,128)(2,1)}), bf16[32,128,128]{2,1,0:T(8,128)(2,1)S(1)}, u32[]{:S(2)}, u32[]{:S(2)}) async-start(bf16[32,128,128]{2,1,0:T(8,128)(2,1)} %bitcast.51), calls=%async_computation.9 | async-start | bytes 2097152 | tf_op jit(solution)/shard_map/all_to_all | solution.py:159
  356.2 2.8 add_convert_fusion.1
  359.0 12.5 %all-to-all-done.9 = bf16[32,128,128]{2,1,0:T(8,128)(2,1)S(1)} async-done(((bf16[32,128,128]{2,1,0:T(8,128)(2,1)}), bf16[32,128,128]{2,1,0:T(8,128)(2,1)S(1)}, u32[]{:S(2)}, u32[]{:S(2)}) %all-to-all-start.9) | async-done | bytes 1048608 | tf_op jit(solution)/shard_map/all_to_all | solution.py:159
  371.5 4.0 %all-to-all-start.8 = ((bf16[32,128,128]{2,1,0:T(8,128)(2,1)}), bf16[32,128,128]{2,1,0:T(8,128)(2,1)S(1)}, u32[]{:S(2)}, u32[]{:S(2)}) async-start(bf16[32,128,128]{2,1,0:T(8,128)(2,1)} %bitcast.47), calls=%async_computation.8 | async-start | bytes 2097152 | tf_op jit(solution)/shard_map/all_to_all | solution.py:158
  375.4 2.3 copy.73
  377.7 2.3 copy.80
  381.2 11.2 %all-to-all-done.8 = bf16[32,128,128]{2,1,0:T(8,128)(2,1)S(1)} async-done(((bf16[32,128,128]{2,1,0:T(8,128)(2,1)}), bf16[32,128,128]{2,1,0:T(8,128)(2,1)S(1)}, u32[]{:S(2)}, u32[]{:S(2)}) %all-to-all-start.8) | async-done | bytes 1048608 | tf_op jit(solution)/shard_map/all_to_all | solution.py:158
  (214 shorter events, 109.0 us)
Async XLA Ops:
  0.6 96.9 %copy-start = (bf16[128,4096]{1,0:T(8,128)(2,1)S(1)}, bf16[128,4096]{1,0:T(8,128)(2,1)}, u32[]{:S(2)}) copy-start(bf16[128,4096]{1,0:T(8,128)(2,1)} %param.8) | copy-start | bytes 3145732
  0.6 23.7 %copy-start.1 = (bf16[128,1024]{1,0:T(8,128)(2,1)S(1)}, bf16[128,1024]{1,0:T(8,128)(2,1)}, u32[]{:S(2)}) copy-start(bf16[128,1024]{1,0:T(8,128)(2,1)} %param.9) | copy-start | bytes 786436
  8.5 40.0 %copy-start.3 = (bf16[128,4096]{1,0:T(8,128)(2,1)S(1)}, bf16[128,4096]{1,0:T(8,128)(2,1)}, u32[]{:S(2)}) copy-start(bf16[128,4096]{1,0:T(8,128)(2,1)} %param.11) | copy-start | bytes 3145732
  8.5 29.0 %all-to-all-start.5 = ((bf16[16,8,1024]{2,1,0:T(8,128)(2,1)}), bf16[16,8,1024]{2,1,0:T(8,128)(2,1)S(1)}, u32[]{:S(2)}, u32[]{:S(2)}) async-start(bf16[16,8,1024]{2,1,0:T(8,128)(2,1)} %bitcast.37), calls=%async_computation.5 | async-start | bytes 524288 | tf_op jit(solution)/shard_map/all_to_all | solution.py:146
  37.5 24.0 %all-to-all-start = ((bf16[16,8,1024]{2,1,0:T(8,128)(2,1)}), bf16[16,8,1024]{2,1,0:T(8,128)(2,1)S(1)}, u32[]{:S(2)}, u32[]{:S(2)}) async-start(bf16[16,8,1024]{2,1,0:T(8,128)(2,1)} %bitcast.23), calls=%async_computation | async-start | bytes 524288 | tf_op jit(solution)/shard_map/all_to_all | solution.py:145
  61.5 30.4 %all-to-all-start.4 = ((bf16[128,32,128]{0,2,1:T(8,128)(2,1)}), bf16[128,32,128]{0,2,1:T(8,128)(2,1)S(1)}, u32[]{:S(2)}, u32[]{:S(2)}) async-start(bf16[128,32,128]{0,2,1:T(8,128)(2,1)} %bitcast.34), calls=%async_computation.4 | async-start | bytes 2097152 | tf_op jit(solution)/shard_map/all_to_all | solution.py:152
  93.1 21.4 %all-to-all-start.1 = ((bf16[128,32,128]{2,0,1:T(8,128)(2,1)}), bf16[128,32,128]{2,0,1:T(8,128)(2,1)}, u32[]{:S(2)}, u32[]{:S(2)}) async-start(bf16[128,32,128]{2,0,1:T(8,128)(2,1)} %bitcast.24), calls=%async_computation.1 | async-start | bytes 2097152 | tf_op jit(solution)/shard_map/all_to_all | solution.py:150
  114.5 51.8 %all-to-all-start.2 = ((bf16[16,8,4096]{2,1,0:T(8,128)(2,1)}), bf16[16,8,4096]{2,1,0:T(8,128)(2,1)S(1)}, u32[]{:S(2)}, u32[]{:S(2)}) async-start(bf16[16,8,4096]{2,1,0:T(8,128)(2,1)} %bitcast.30), calls=%async_computation.2 | async-start | bytes 2097152 | tf_op jit(solution)/shard_map/all_to_all | solution.py:144
  167.6 25.8 %all-to-all-start.6 = ((bf16[128,32,128]{2,0,1:T(8,128)(2,1)}), bf16[128,32,128]{2,0,1:T(8,128)(2,1)}, u32[]{:S(2)}, u32[]{:S(2)}) async-start(bf16[128,32,128]{2,0,1:T(8,128)(2,1)} %bitcast.38), calls=%async_computation.6 | async-start | bytes 2097152 | tf_op jit(solution)/shard_map/all_to_all | solution.py:151
  176.6 21.3 %copy-start.4 = (s32[1,128]{1,0:T(1,128)S(1)}, s32[1,128]{1,0:T(1,128)}, u32[]{:S(2)}) copy-start(s32[1,128]{1,0:T(1,128)} %param.13) | copy-start | bytes 1540
  193.3 41.5 %all-to-all-start.3 = ((bf16[128,32,128]{2,0,1:T(8,128)(2,1)}), bf16[128,32,128]{2,0,1:T(8,128)(2,1)}, u32[]{:S(2)}, u32[]{:S(2)}) async-start(bf16[128,32,128]{2,0,1:T(8,128)(2,1)} %copy.62), calls=%async_computation.3 | async-start | bytes 2097152 | tf_op jit(solution)/shard_map/all_to_all | solution.py:149
  327.8 21.8 %all-to-all-start.7 = ((bf16[32,128,128]{2,1,0:T(8,128)(2,1)}), bf16[32,128,128]{2,1,0:T(8,128)(2,1)S(1)}, u32[]{:S(2)}, u32[]{:S(2)}) async-start(bf16[32,128,128]{2,1,0:T(8,128)(2,1)} %bitcast.165), calls=%async_computation.7 | async-start | bytes 2097152 | tf_op jit(solution)/shard_map/all_to_all | solution.py:157
  349.6 1.0 copy-start.2
  350.6 20.9 %all-to-all-start.9 = ((bf16[32,128,128]{2,1,0:T(8,128)(2,1)}), bf16[32,128,128]{2,1,0:T(8,128)(2,1)S(1)}, u32[]{:S(2)}, u32[]{:S(2)}) async-start(bf16[32,128,128]{2,1,0:T(8,128)(2,1)} %bitcast.51), calls=%async_computation.9 | async-start | bytes 2097152 | tf_op jit(solution)/shard_map/all_to_all | solution.py:159
  371.5 20.9 %all-to-all-start.8 = ((bf16[32,128,128]{2,1,0:T(8,128)(2,1)}), bf16[32,128,128]{2,1,0:T(8,128)(2,1)S(1)}, u32[]{:S(2)}, u32[]{:S(2)}) async-start(bf16[32,128,128]{2,1,0:T(8,128)(2,1)} %bitcast.47), calls=%async_computation.8 | async-start | bytes 2097152 | tf_op jit(solution)/shard_map/all_to_all | solution.py:158
where the time goes:
time: 396 us; the launch traced here: 394 us
  waiting for transfers between devices  153 us (39%)
  local copies, waits for them, and re-layouts  76.4 us (19%)
  starting transfers between devices  76.1 us (19%)
  matrix products  37.1 us (9%)
  blocking collectives  29.8 us (8%)
  other arithmetic  19.9 us (5%)
    all_to_all x1, waiting for transfers between devices, body(): lax.all_to_all(query_rows[row_order], 'dp', split_axis=0, concat_axis=0,...  46.3 us
    all_gather x1, blocking collectives, body(): seg_all = lax.all_gather(segments, 'seq', axis=1, tiled=True)[0]  29.8 us
    dynamic_update_slice x48, local copies, waits for them, and re-layouts, band_pass(): lax.scan(block_step, jnp.int32(0), (query_blocks, key_prior, key_blocks,...  22.8 us
    all_to_all x1, waiting for transfers between devices, body(): lax.all_to_all(grad_rows, 'seq', split_axis=1, concat_axis=0, tiled=True)  16.8 us
    squeeze x16, local copies, waits for them, and re-layouts, band_pass(): lax.scan(block_step, jnp.int32(0), (query_blocks, key_prior, key_blocks,...  15.9 us
    all_to_all x1, starting transfers between devices, body(): lax.all_to_all(source_value_rows[row_order], 'dp', split_axis=0, concat_a...  15.9 us
    all_to_all x1, waiting for transfers between devices, body(): lax.all_to_all(widen_heads(moved_v), 'seq', split_axis=1, concat_axis=0,...  15.4 us
    all_to_all x1, waiting for transfers between devices, body(): lax.all_to_all(widen_heads(moved_k), 'seq', split_axis=1, concat_axis=0,...  14.8 us
  transfers between devices with their start and end apart: 10, of which 9 were waited for; matrix products, arithmetic and copies ran while one was open for 7% of the time, Pallas kernels for 0%

commit v1 on v0

v1 whole, which is shorter than its diff:
```python
import functools

import jax
import jax.numpy as jnp
from jax import lax
from jax.experimental import pallas as pl
from jax.experimental.pallas import tpu as pltpu
from jax.sharding import PartitionSpec as P

MESH = pl.DeviceIdType.MESH
D = 128
GROUP = 4
CHUNKS = 4
NZ = 16
NC = 16
CAP = 8
ROWS = 2 * D
BAND = 5 * D
WIDE = GROUP * D
SCALE = D ** (-0.5)
LOG2E = 1.4426950408889634
NEG = -1e30
F32, BF16 = jnp.float32, jnp.bfloat16


def dot(a, b, ca, cb):
    return lax.dot_general(a, b, (((ca,), (cb,)), ((), ())), preferred_element_type=F32)


def kernel(
    q_ref, k_ref, v_ref, g_ref, routes_ref, seg_ref,
    dq_out, dk_out, dv_out,
    kv_send, kv_recv, q_send, q_recv, g_buf, band, seg_src, seg_band, bias,
    acc_k, acc_v, own, part_send, part_recv, dq_stage, dq_recv, dkv_send, dkv_recv,
    kv_ss, kv_rs, q_ss, q_rs, g_ss, g_rs, seg_ss, seg_rs, halo_ss, halo_rs,
    part_ss, part_rs, dq_ss, dq_rs, dkv_ss, dkv_rs,
):
    z = lax.axis_index("dp")
    s = lax.axis_index("seq")
    c, core = s // 2, s % 2
    other = 1 - core

    def at(dz, dc, to_core):
        return {"dp": (z + dz + NZ) % NZ, "seq": ((c + dc + NC) % NC) * 2 + to_core}

    def remote(src, dst, ssem, rsem, device):
        return pltpu.make_async_remote_copy(
            src_ref=src, dst_ref=dst, send_sem=ssem, recv_sem=rsem,
            device_id=device, device_id_type=MESH,
        )

    def drain(ref, sem):
        pltpu.make_async_copy(ref, ref, sem).wait()

    def step_of(i):
        return (i // 2 + 1) * (1 - 2 * (i % 2))

    barrier = pltpu.get_barrier_semaphore()

    def greet(dz, dc, to_core):
        pl.semaphore_signal(barrier, inc=1, device_id=at(dz, dc, to_core), device_id_type=MESH)

    def greet_z(i, carry):
        greet(step_of(i), 0, core)
        greet(step_of(i), 0, other)
        return carry

    lax.fori_loop(0, NZ - 1, greet_z, 0)
    greet(0, 0, other)
    for dc in (1, 2, -1, -2):
        greet(0, dc, core)
        greet(0, dc, other)

    lane = lax.broadcasted_iota(jnp.int32, (D, D), 1)
    sub = lax.broadcasted_iota(jnp.int32, (D, D), 0)
    routes = routes_ref[...]
    onehot = (routes == lane).astype(F32)
    before = dot((lane < sub).astype(BF16), onehot.astype(BF16), 1, 0)
    rank = jnp.sum(before * onehot, axis=1, keepdims=True)
    slot = routes.astype(F32) * float(CAP) + rank
    order = (slot == lane.astype(F32)).astype(F32).T.astype(BF16)

    def permuted(ref, start):
        moved = dot(order, ref[:, start : start + WIDE], 1, 0)
        return moved.reshape(NZ, CAP, WIDE).astype(BF16)

    for h in range(2):
        kv_send[h * NZ : (h + 1) * NZ, :, :WIDE] = permuted(k_ref, h * WIDE)
        kv_send[h * NZ : (h + 1) * NZ, :, WIDE:] = permuted(v_ref, h * WIDE)
    seg_src[...] = jnp.broadcast_to(seg_ref[...], seg_src.shape)

    pl.semaphore_wait(barrier, 2 * (NZ - 1) + 1 + 8)

    def scatter(send, recv, ssem, rsem):
        here = core * NZ + z

        def step(i, carry):
            d = step_of(i)
            r = (z + d + NZ) % NZ
            for to_core in (core, other):
                remote(send.at[to_core * NZ + r], recv.at[here], ssem, rsem, at(d, 0, to_core)).start()
            return carry

        lax.fori_loop(0, NZ - 1, step, 0)
        remote(send.at[other * NZ + z], recv.at[here], ssem, rsem, at(0, 0, other)).start()
        pltpu.make_async_copy(send.at[core * NZ + z], recv.at[here], rsem).start()

    scatter(kv_send, kv_recv, kv_ss, kv_rs)

    for j in range(CHUNKS):
        for h in range(2):
            q_send[j, h * NZ : (h + 1) * NZ] = permuted(q_ref, (h * CHUNKS + j) * WIDE)
        scatter(q_send.at[j], q_recv.at[j], q_ss.at[j], q_rs.at[j])

    half = CHUNKS * WIDE
    remote(
        g_ref.at[:, pl.ds(pl.multiple_of(other * half, half), half)], g_buf.at[core], g_ss, g_rs, at(0, 0, other)
    ).start()
    pltpu.make_async_copy(g_ref.at[:, pl.ds(pl.multiple_of(core * half, half), half)], g_buf.at[core], g_rs).start()
    remote(seg_src, seg_band.at[4 + core], seg_ss, seg_rs, at(0, 0, other)).start()
    pltpu.make_async_copy(seg_src, seg_band.at[4 + core], seg_rs).start()
    for dc in (1, 2):
        for to_core in (core, other):
            remote(seg_src, seg_band.at[4 - 2 * dc + core], seg_ss, seg_rs, at(0, dc, to_core)).start()

    drain(seg_band, seg_rs)
    for t in range(2):
        seg_q = seg_band[4 + t, 0:1, :].astype(F32)
        for b in range(5):
            seg_k = jnp.broadcast_to(seg_band[t + b, 0:1, :].astype(F32), (D, D)).T
            allowed = seg_k == seg_q
            if b == 4:
                allowed = allowed & (sub <= lane)
            if t + b < 4:
                allowed = allowed & (sub + ((t + b) * D - 2 * ROWS + c * ROWS) >= 0)
            bias[t, b * D : (b + 1) * D, :] = jnp.where(allowed, 0.0, NEG)

    drain(kv_recv, kv_rs)
    band[2 * ROWS :, :] = kv_recv[...].astype(F32).reshape(ROWS, 2 * WIDE).astype(BF16)
    mine = band.at[pl.ds(2 * ROWS, ROWS)]
    for dc in (1, 2):
        remote(mine, band.at[pl.ds((2 - dc) * ROWS, ROWS)], halo_ss, halo_rs, at(0, dc, core)).start()
    drain(g_buf, g_rs)
    drain(band.at[pl.ds(0, 2 * ROWS)], halo_rs)

    def chunk(j, carry):
        drain(q_recv.at[j], q_rs.at[j])
        k_at = pl.ds(pl.multiple_of(j * D, D), D)
        v_at = pl.ds(pl.multiple_of(WIDE + j * D, D), D)
        acc_k[BAND:, :] = jnp.zeros((D, D), F32)
        acc_v[BAND:, :] = jnp.zeros((D, D), F32)
        for t in range(2):
            keys = band[t * D : t * D + BAND, k_at]
            values = band[t * D : t * D + BAND, v_at]
            q_rows = q_recv[j, t * NZ : (t + 1) * NZ].astype(F32).reshape(D, WIDE).astype(BF16)
            g_rows = g_buf[t, :, pl.ds(pl.multiple_of(j * WIDE, WIDE), WIDE)]
            queries = jnp.concatenate([q_rows[:, a * D : (a + 1) * D] for a in range(GROUP)], axis=0)
            grads = jnp.concatenate([g_rows[:, a * D : (a + 1) * D] for a in range(GROUP)], axis=0)
            masked = jnp.concatenate([bias[t]] * GROUP, axis=1)
            score = dot(keys, queries, 1, 1) * (SCALE * LOG2E) + masked
            weight = jnp.exp2(score - jnp.max(score, axis=0, keepdims=True))
            prob = weight * (1.0 / jnp.sum(weight, axis=0, keepdims=True))
            prob_low = prob.astype(BF16)
            grad_prob = dot(values, grads, 1, 1)
            delta = jnp.sum(prob_low.astype(F32) * grad_prob, axis=0, keepdims=True)
            grad_score = (prob * (grad_prob - delta) * SCALE).astype(BF16)
            dk = dot(grad_score, queries, 1, 0)
            dv = dot(prob_low, grads, 1, 0)
            if t == 0:
                acc_k[:BAND, :] = dk
                acc_v[:BAND, :] = dv
            else:
                acc_k[D:, :] += dk
                acc_v[D:, :] += dv
            dq = dot(keys, grad_score, 0, 0)
            for a in range(GROUP):
                dq_stage[j, t, :, a * D : (a + 1) * D] = dq[:, a * D : (a + 1) * D].T.astype(BF16)
        for b in range(2):
            part_send[j, b, :, :D] = acc_k[b * ROWS : (b + 1) * ROWS, :].astype(BF16)
            part_send[j, b, :, D:] = acc_v[b * ROWS : (b + 1) * ROWS, :].astype(BF16)
            remote(part_send.at[j, b], part_recv.at[j, b], part_ss.at[j], part_rs.at[j], at(0, b - 2, core)).start()
        own[j, :, :D] = acc_k[2 * ROWS :, :]
        own[j, :, D:] = acc_v[2 * ROWS :, :]
        remote(dq_stage.at[j, other], dq_recv.at[j], dq_ss.at[j], dq_rs.at[j], at(0, 0, other)).start()
        return carry

    lax.fori_loop(0, CHUNKS, chunk, 0)

    def fold(j, carry):
        drain(part_recv.at[j], part_rs.at[j])
        total = own[j] + part_recv[j, 0].astype(F32) + part_recv[j, 1].astype(F32)
        dkv_send[j] = total.reshape(2, D, 2 * D).astype(BF16)
        remote(dkv_send.at[j, other], dkv_recv.at[j], dkv_ss.at[j], dkv_rs.at[j], at(0, 0, other)).start()
        return carry

    lax.fori_loop(0, CHUNKS, fold, 0)
    for j in range(CHUNKS):
        dq_out[core, :, j * WIDE : (j + 1) * WIDE] = dq_stage[j, core]
        dk_out[core, :, j * D : (j + 1) * D] = dkv_send[j, core, :, :D]
        dv_out[core, :, j * D : (j + 1) * D] = dkv_send[j, core, :, D:]
    for j in range(CHUNKS):
        drain(dq_recv.at[j], dq_rs.at[j])
        dq_out[other, :, j * WIDE : (j + 1) * WIDE] = dq_recv[j]
        drain(dkv_recv.at[j], dkv_rs.at[j])
        dk_out[other, :, j * D : (j + 1) * D] = dkv_recv[j, :, :D]
        dv_out[other, :, j * D : (j + 1) * D] = dkv_recv[j, :, D:]

    drain(kv_send.at[pl.ds(0, 2 * NZ - 1)], kv_ss)
    drain(g_buf.at[0], g_ss)
    drain(seg_band.at[pl.ds(0, 5)], seg_ss)
    drain(band.at[pl.ds(0, 2 * ROWS)], halo_ss)
    for j in range(CHUNKS):
        drain(q_send.at[j, pl.ds(0, 2 * NZ - 1)], q_ss.at[j])
        drain(part_send.at[j], part_ss.at[j])
        drain(dq_recv.at[j], dq_ss.at[j])
        drain(dkv_recv.at[j], dkv_ss.at[j])


def body(query_rows, source_key_rows, source_value_rows, grad_rows, routes, segments):
    dma = pltpu.SemaphoreType.DMA
    vmem = pltpu.VMEM
    call = pl.pallas_call(
        kernel,
        out_shape=(
            jax.ShapeDtypeStruct((2, D, CHUNKS * WIDE), BF16),
            jax.ShapeDtypeStruct((2, D, CHUNKS * D), BF16),
            jax.ShapeDtypeStruct((2, D, CHUNKS * D), BF16),
        ),
        in_specs=[pl.BlockSpec(memory_space=vmem)] * 6,
        out_specs=[pl.BlockSpec(memory_space=vmem)] * 3,
        scratch_shapes=[
            vmem((2 * NZ, CAP, 2 * WIDE), BF16),
            vmem((2 * NZ, CAP, 2 * WIDE), BF16),
            vmem((CHUNKS, 2 * NZ, CAP, WIDE), BF16),
            vmem((CHUNKS, 2 * NZ, CAP, WIDE), BF16),
            vmem((2, D, CHUNKS * WIDE), BF16),
            vmem((3 * ROWS, 2 * WIDE), BF16),
            vmem((8, D), jnp.int32),
            vmem((6, 8, D), jnp.int32),
            vmem((2, BAND, D), F32),
            vmem((3 * ROWS, D), F32),
            vmem((3 * ROWS, D), F32),
            vmem((CHUNKS, ROWS, 2 * D), F32),
            vmem((CHUNKS, 2, ROWS, 2 * D), BF16),
            vmem((CHUNKS, 2, ROWS, 2 * D), BF16),
            vmem((CHUNKS, 2, D, WIDE), BF16),
            vmem((CHUNKS, D, WIDE), BF16),
            vmem((CHUNKS, 2, D, 2 * D), BF16),
            vmem((CHUNKS, D, 2 * D), BF16),
            dma, dma, dma((CHUNKS,)), dma((CHUNKS,)), dma, dma, dma, dma, dma, dma,
            dma((CHUNKS,)), dma((CHUNKS,)), dma((CHUNKS,)), dma((CHUNKS,)), dma((CHUNKS,)), dma((CHUNKS,)),
        ],
        compiler_params=pltpu.CompilerParams(
            collective_id=0, has_side_effects=True, vmem_limit_bytes=56 << 20
        ),
    )
    dq, dk, dv = call(query_rows, source_key_rows, source_value_rows, grad_rows, routes, segments)

    def rows_first(halves):
        return halves.transpose(1, 0, 2).reshape(halves.shape[1], -1)

    return rows_first(dq), rows_first(dk), rows_first(dv)


def solution(mesh):
    placed = (P(("dp", "seq"), None),) * 5 + (P("dp", "seq"),)
    return jax.shard_map(
        body,
        mesh=mesh,
        in_specs=placed,
        out_specs=(P(("dp", "seq"), None),) * 3,
        check_vma=False,
    )
```

time: 396 us -> 119 us (0.30)
  the two profiles are of different devices: /device:TPU:1 before, /device:TPU:37 now
where the time goes in v1:
time: 119 us
  Pallas kernels  112 us (94%)
  local copies, waits for them, and re-layouts  6.46 us (5%)
    pallas_call x1, Pallas kernels, body(): call(query_rows, source_key_rows, source_value_rows, grad_rows, routes, s...  112 us
    unnamed x8, local copies, waits for them, and re-layouts  4.51 us

profile of v1, /device:TPU:37, one launch (start us, length us, event | category | flops | bytes accessed | tf_op | source)
XLA Modules:
  0.0 118.9 jit_solution(4714186217767852734)
XLA Ops:
  0.6 1.4 %copy.10.routes_ref = s32[128,1]{1,0:T(8,128)} copy(s32[128,1]{0,1:T(1,128)} %param.10) | data formatting | bytes 1024 | tf_op args[4]
  2.0 111.7 %shard_map.85 = (bf16[2,128,2048]{2,1,0:T(8,128)(2,1)}, bf16[2,128,512]{2,1,0:T(8,128)(2,1)}, bf16[2,128,512]{2,1,0:T(8,128)(2,1)}) custom-call(bf16[128,4096]{1,0:T(8,128)(2,1)} %q_ref.1, bf16[128,1024]{1,0:T(8,128)(2,1)} %k_ref.1, bf16[128,1024]{1,0:T(8,128)(2,1)} %v_ref.1, bf16[128,4096]{1,0:T(8,128)(2,1)} %g_ref.1, s32[128,1]{1,0:T(8,128)} %copy.10.routes_ref, ...), custom_call_target="tpu_custom_call" | custom-call | tf_op jit(solution)/shard_map/pallas_call | solution.py:257
  113.8 1.6 %copy.11 = bf16[128,2,2048]{0,2,1:T(8,128)(2,1)S(1)} copy(bf16[128,2,2048]{2,0,1:T(8,128)(2,1)} %bitcast.7) | data formatting | bytes 2097152 | tf_op jit(solution)/shard_map/transpose | solution.py:260
  115.4 0.0 copy-start.1
  115.4 1.3 %copy.14 = bf16[128,4096]{1,0:T(8,128)(2,1)} copy(bf16[128,4096]{0,1:T(8,128)(2,1)S(1)} %bitcast.6) | data formatting | bytes 2097152
  116.7 0.0 copy-done.1
  116.7 0.2 copy.12
  116.9 0.0 copy-start
  116.9 0.9 copy.15
  117.7 0.1 copy-done
  117.8 0.2 copy.13
  118.0 0.9 copy.16
Async XLA Ops:
  115.4 1.3 %copy-start.1 = (bf16[2,128,512]{2,1,0:T(8,128)(2,1)S(1)}, bf16[2,128,512]{2,1,0:T(8,128)(2,1)}, u32[]{:S(2)}) copy-start(bf16[2,128,512]{2,1,0:T(8,128)(2,1)} %get-tuple-element.7) | copy-start | bytes 786436
  116.9 1.0 copy-start

commit v2 on v1

v2 whole, which is shorter than its diff:
```python
import functools

import jax
import jax.numpy as jnp
from jax import lax
from jax.experimental import pallas as pl
from jax.experimental.pallas import tpu as pltpu
from jax.sharding import PartitionSpec as P

MESH = pl.DeviceIdType.MESH
D = 128
GROUP = 4
CHUNKS = 4
NZ = 16
NC = 16
CAP = 8
ROWS = 2 * D
BAND = 5 * D
WIDE = GROUP * D
SCALE = D ** (-0.5)
LOG2E = 1.4426950408889634
NEG = -1e30
F32, BF16 = jnp.float32, jnp.bfloat16


def dot(a, b, ca, cb):
    return lax.dot_general(a, b, (((ca,), (cb,)), ((), ())), preferred_element_type=F32)


def kernel(
    q_hbm, k_hbm, v_hbm, g_hbm, routes_ref, seg_ref,
    dq_out, dk_out, dv_out,
    q_in, kv_in, kv_send, kv_recv, q_send, q_recv, g_buf, band, seg_src, seg_band, bias,
    acc, part_send, part_recv, dq_stage,
    in_s, kv_ss, kv_rs, q_ss, q_rs, g_ss, g_rs, seg_ss, seg_rs, halo_ss, halo_rs,
    part_ss, part_rs, dq_ss, dq_rs,
):
    z = lax.axis_index("dp")
    s = lax.axis_index("seq")
    c, core = s // 2, s % 2
    other = 1 - core
    half = CHUNKS * WIDE

    def at(dz, dc, to_core):
        return {"dp": lax.rem(z + dz + NZ, NZ), "seq": lax.rem(c + dc + NC, NC) * 2 + to_core}

    def remote(src, dst, ssem, rsem, device):
        return pltpu.make_async_remote_copy(
            src_ref=src, dst_ref=dst, send_sem=ssem, recv_sem=rsem,
            device_id=device, device_id_type=MESH,
        )

    def drain(ref, sem):
        pltpu.make_async_copy(ref, ref, sem).wait()

    def columns(start, size):
        return pl.ds(pl.multiple_of(start, size), size)

    def step_of(i):
        return (i // 2 + 1) * (1 - 2 * (i % 2))

    loads = [
        pltpu.make_async_copy(k_hbm, kv_in.at[0], in_s.at[0]),
        pltpu.make_async_copy(v_hbm, kv_in.at[1], in_s.at[1]),
        pltpu.make_async_copy(q_hbm, q_in, in_s.at[2]),
    ]
    for load in loads:
        load.start()

    barrier = pltpu.get_barrier_semaphore()

    def greet(dz, dc, to_core):
        pl.semaphore_signal(barrier, inc=1, device_id=at(dz, dc, to_core), device_id_type=MESH)

    def greet_z(i, carry):
        greet(step_of(i), 0, core)
        greet(step_of(i), 0, other)
        return carry

    lax.fori_loop(0, NZ - 1, greet_z, 0)
    greet(0, 0, other)
    for dc in (1, 2, -1, -2):
        greet(0, dc, core)
        greet(0, dc, other)

    lane = lax.broadcasted_iota(jnp.int32, (D, D), 1)
    sub = lax.broadcasted_iota(jnp.int32, (D, D), 0)
    routes = routes_ref[...]
    onehot = (routes == sub).astype(F32)
    before = dot(onehot.astype(BF16), (sub < lane).astype(BF16), 1, 0)
    rank = jnp.sum(before * onehot, axis=0, keepdims=True)
    slot = routes.astype(F32) * float(CAP) + rank
    order = (slot == sub.astype(F32)).astype(BF16)

    def permuted(rows):
        return dot(order, rows, 1, 0).reshape(NZ, CAP, WIDE).astype(BF16)

    for i in range(2):
        loads[i].wait()
        for h in range(2):
            moved = permuted(kv_in[i, :, h * WIDE : (h + 1) * WIDE])
            for j in range(CHUNKS):
                first = (2 * j + i) * D
                kv_send[h * NZ : (h + 1) * NZ, :, first : first + D] = moved[:, :, j * D : (j + 1) * D]

    pl.semaphore_wait(barrier, 2 * (NZ - 1) + 1 + 8)

    def scatter(send, recv, ssem, rsem):
        here = core * NZ + z

        def step(i, carry):
            d = step_of(NZ - 2 - i)
            r = lax.rem(z + d + NZ, NZ)
            for to_core in (core, other):
                remote(send.at[to_core * NZ + r], recv.at[here], ssem, rsem, at(d, 0, to_core)).start()
            return carry

        lax.fori_loop(0, NZ - 1, step, 0)
        remote(send.at[other * NZ + z], recv.at[here], ssem, rsem, at(0, 0, other)).start()
        pltpu.make_async_copy(send.at[core * NZ + z], recv.at[here], rsem).start()

    scatter(kv_send, kv_recv, kv_ss, kv_rs)

    loads[2].wait()
    for j in range(CHUNKS):
        for h in range(2):
            first = (h * CHUNKS + j) * WIDE
            q_send[j, h * NZ : (h + 1) * NZ] = permuted(q_in[:, first : first + WIDE])

    def send_queries(j, carry):
        scatter(q_send.at[j], q_recv.at[j], q_ss.at[j], q_rs.at[j])
        return carry

    lax.fori_loop(0, 4, send_queries, 0)
    seg_src[...] = jnp.broadcast_to(seg_ref[...], seg_src.shape)
    remote(seg_src, seg_band.at[4 + core], seg_ss, seg_rs, at(0, 0, other)).start()
    pltpu.make_async_copy(seg_src, seg_band.at[4 + core], seg_rs).start()
    for dc in (1, 2):
        for to_core in (core, other):
            remote(seg_src, seg_band.at[4 - 2 * dc + core], seg_ss, seg_rs, at(0, dc, to_core)).start()
    remote(g_hbm.at[:, columns(other * half, half)], g_buf.at[core], g_ss, g_rs, at(0, 0, other)).start()
    pltpu.make_async_copy(g_hbm.at[:, columns(core * half, half)], g_buf.at[core], g_rs).start()

    drain(seg_band, seg_rs)
    for t in range(2):
        seg_q = seg_band[4 + t, 0:1, :].astype(F32)
        for b in range(5):
            seg_k = jnp.broadcast_to(seg_band[t + b, 0:1, :].astype(F32), (D, D)).T
            allowed = seg_k == seg_q
            if b == 4:
                allowed = allowed & (sub <= lane)
            if t + b < 4:
                allowed = allowed & (sub + ((t + b) * D - 2 * ROWS + c * ROWS) >= 0)
            bias[t, b * D : (b + 1) * D, :] = jnp.where(allowed, 0.0, NEG)

    drain(kv_recv, kv_rs)
    for j in range(CHUNKS):
        rows = kv_recv[:, :, 2 * j * D : 2 * (j + 1) * D].astype(F32).reshape(ROWS, 2 * D)
        band[j, 2 * ROWS :, :] = rows.astype(BF16)
        mine = band.at[j, pl.ds(2 * ROWS, ROWS)]
        for dc in (1, 2):
            remote(mine, band.at[j, pl.ds((2 - dc) * ROWS, ROWS)], halo_ss.at[j], halo_rs.at[j], at(0, dc, core)).start()
    drain(g_buf, g_rs)

    def send_part(j, b):
        to = part_recv.at[j, 2 - b // 2, core]
        remote(part_send.at[j, b], to, part_ss.at[j], part_rs.at[j], at(0, b // 2 - 2, b % 2)).start()

    def chunk(j):
        drain(band.at[j, pl.ds(0, 2 * ROWS)], halo_rs.at[j])
        drain(q_recv.at[j], q_rs.at[j])
        for t in range(2):
            keys = band[j, t * D : t * D + BAND, :D]
            values = band[j, t * D : t * D + BAND, D:]
            q_rows = q_recv[j, t * NZ : (t + 1) * NZ].astype(F32).reshape(D, WIDE).astype(BF16)
            g_rows = g_buf[t, :, columns(j * WIDE, WIDE)]
            queries = jnp.concatenate([q_rows[:, a * D : (a + 1) * D] for a in range(GROUP)], axis=0)
            grads = jnp.concatenate([g_rows[:, a * D : (a + 1) * D] for a in range(GROUP)], axis=0)
            masked = jnp.concatenate([bias[t]] * GROUP, axis=1)
            score = dot(keys, queries, 1, 1) * (SCALE * LOG2E) + masked
            weight = jnp.exp2(score - jnp.max(score, axis=0, keepdims=True))
            prob = weight * (1.0 / jnp.sum(weight, axis=0, keepdims=True))
            prob_low = prob.astype(BF16)
            grad_prob = dot(values, grads, 1, 1)
            delta = jnp.sum(prob_low.astype(F32) * grad_prob, axis=0, keepdims=True)
            grad_score = (prob * (grad_prob - delta) * SCALE).astype(BF16)
            dk = dot(grad_score, queries, 1, 0)
            dv = dot(prob_low, grads, 1, 0)
            dq = dot(keys, grad_score, 0, 0)
            for a in range(GROUP):
                dq_stage[j, t, :, a * D : (a + 1) * D] = dq[:, a * D : (a + 1) * D].T.astype(BF16)
            if t == 0:
                acc[:, :D] = dk
                acc[:, D:] = dv
                part_send[j, 0, :, :D] = dk[:D].astype(BF16)
                part_send[j, 0, :, D:] = dv[:D].astype(BF16)
                send_part(j, 0)
            else:
                for b in range(1, 6):
                    rows = slice(b * D, (b + 1) * D)
                    if b < 5:
                        k_sum, v_sum = acc[rows, :D], acc[rows, D:]
                    k_new, v_new = dk[(b - 1) * D : b * D], dv[(b - 1) * D : b * D]
                    k_sum = k_new if b == 5 else k_sum + k_new
                    v_sum = v_new if b == 5 else v_sum + v_new
                    part_send[j, b, :, :D] = k_sum.astype(BF16)
                    part_send[j, b, :, D:] = v_sum.astype(BF16)
        for b in range(1, 4):
            send_part(j, b)
        remote(part_send.at[j, 4 + other], part_recv.at[j, 0, core], part_ss.at[j], part_rs.at[j], at(0, 0, other)).start()
        pltpu.make_async_copy(part_send.at[j, 4 + core], part_recv.at[j, 0, core], part_rs.at[j]).start()
        to = dq_out.at[:, columns(core * half + j * WIDE, WIDE)]
        remote(dq_stage.at[j, other], to, dq_ss.at[j], dq_rs.at[j], at(0, 0, other)).start()
        pltpu.make_async_copy(dq_stage.at[j, core], to, dq_rs.at[j]).start()

    def fold(j):
        drain(part_recv.at[j], part_rs.at[j])
        for h in range(2):
            total = part_recv[j, 0, h].astype(F32) + part_recv[j, 1, h].astype(F32) + part_recv[j, 2, h].astype(F32)
            total = total.astype(BF16)
            dk_out[:, columns(h * WIDE + j * D, D)] = total[:, :D]
            dv_out[:, columns(h * WIDE + j * D, D)] = total[:, D:]

    def turn(j, carry):
        chunk(j)

        @pl.when(j > 0)
        def _():
            fold(j - 1)

        return carry

    lax.fori_loop(0, CHUNKS, turn, 0)
    fold(CHUNKS - 1)

    drain(kv_send.at[pl.ds(0, 2 * NZ - 1)], kv_ss)
    drain(g_buf.at[0], g_ss)
    drain(seg_band.at[pl.ds(0, 5)], seg_ss)
    for j in range(CHUNKS):
        drain(q_send.at[j, pl.ds(0, 2 * NZ - 1)], q_ss.at[j])
        drain(part_send.at[j, pl.ds(0, 5)], part_ss.at[j])
        drain(band.at[j, pl.ds(0, 2 * ROWS)], halo_ss.at[j])
        drain(dq_stage.at[j, 0], dq_ss.at[j])
        drain(dq_stage.at[j], dq_rs.at[j])


def body(query_rows, source_key_rows, source_value_rows, grad_rows, routes, segments):
    dma = pltpu.SemaphoreType.DMA
    vmem = pltpu.VMEM
    here = pl.BlockSpec(memory_space=vmem)
    apart = pl.BlockSpec(memory_space=pl.ANY)
    return pl.pallas_call(
        kernel,
        out_shape=(
            vmem((D, 2 * CHUNKS * WIDE), BF16),
            vmem((D, 2 * CHUNKS * D), BF16),
            vmem((D, 2 * CHUNKS * D), BF16),
        ),
        in_specs=[apart] * 4 + [here] * 2,
        out_specs=[here] * 3,
        scratch_shapes=[
            vmem((D, 2 * CHUNKS * WIDE), BF16),
            vmem((2, D, 2 * WIDE), BF16),
            vmem((2 * NZ, CAP, 2 * WIDE), BF16),
            vmem((2 * NZ, CAP, 2 * WIDE), BF16),
            vmem((CHUNKS, 2 * NZ, CAP, WIDE), BF16),
            vmem((CHUNKS, 2 * NZ, CAP, WIDE), BF16),
            vmem((2, D, CHUNKS * WIDE), BF16),
            vmem((CHUNKS, 3 * ROWS, 2 * D), BF16),
            vmem((8, D), jnp.int32),
            vmem((6, 8, D), jnp.int32),
            vmem((2, BAND, D), F32),
            vmem((BAND, 2 * D), F32),
            vmem((CHUNKS, 6, D, 2 * D), BF16),
            vmem((CHUNKS, 3, 2, D, 2 * D), BF16),
            vmem((CHUNKS, 2, D, WIDE), BF16),
            dma((3,)), dma, dma, dma((CHUNKS,)), dma((CHUNKS,)), dma, dma, dma, dma, dma((CHUNKS,)), dma((CHUNKS,)),
            dma((CHUNKS,)), dma((CHUNKS,)), dma((CHUNKS,)), dma((CHUNKS,)),
        ],
        compiler_params=pltpu.CompilerParams(
            collective_id=0, has_side_effects=True, vmem_limit_bytes=56 << 20
        ),
    )(query_rows, source_key_rows, source_value_rows, grad_rows, routes.reshape(1, D), segments)


def solution(mesh):
    placed = (P(("dp", "seq"), None),) * 5 + (P("dp", "seq"),)
    return jax.shard_map(
        body,
        mesh=mesh,
        in_specs=placed,
        out_specs=(P(("dp", "seq"), None),) * 3,
        check_vma=False,
    )
```

time: 119 us -> 99.9 us (0.84)
  the two profiles are of different devices: /device:TPU:37 before, /device:TPU:1 now
where the time goes in v2:
time: 99.9 us; the launch traced here: 99.8 us
  Pallas kernels  96.8 us (97%)
  local copies, waits for them, and re-layouts  2.38 us (2%)
    pallas_call x1, Pallas kernels, body(): pl.pallas_call(kernel, out_shape=(vmem((D, 2 * CHUNKS * WIDE), BF16), vme...  96.8 us
    unnamed x3, local copies, waits for them, and re-layouts  2.38 us

profile of v2, /device:TPU:1, one launch (start us, length us, event | category | flops | bytes accessed | tf_op | source)
XLA Modules:
  0.0 99.8 jit_solution(8366365209535516699)
XLA Ops:
  0.6 96.8 %shard_map.85 = (bf16[128,4096]{1,0:T(8,128)(2,1)S(1)}, bf16[128,1024]{1,0:T(8,128)(2,1)S(1)}, bf16[128,1024]{1,0:T(8,128)(2,1)S(1)}) custom-call(bf16[128,4096]{1,0:T(8,128)(2,1)} %q_hbm.1, bf16[128,1024]{1,0:T(8,128)(2,1)} %k_hbm.1, bf16[128,1024]{1,0:T(8,128)(2,1)} %v_hbm.1, bf16[128,4096]{1,0:T(8,128)(2,1)} %g_hbm.1, s32[1,128]{1,0:T(1,128)} %bitcast.1, ...), custom_call_target="tpu_custom_call" | custom-call | tf_op jit(solution)/shard_map/pallas_call | solution.py:252
  97.4 1.0 copy.12
  98.4 0.7 copy.13
  99.1 0.7 copy.14

commit v3 on v2

--- a/solution.py
+++ b/solution.py
@@ -31,7 +31,7 @@
     q_hbm, k_hbm, v_hbm, g_hbm, routes_ref, seg_ref,
     dq_out, dk_out, dv_out,
     q_in, kv_in, kv_send, kv_recv, q_send, q_recv, g_buf, band, seg_src, seg_band, bias,
-    acc, part_send, part_recv, dq_stage,
+    part_send, part_recv, dq_stage,
     in_s, kv_ss, kv_rs, q_ss, q_rs, g_ss, g_rs, seg_ss, seg_rs, halo_ss, halo_rs,
     part_ss, part_rs, dq_ss, dq_rs,
 ):
@@ -105,30 +105,42 @@
 
     pl.semaphore_wait(barrier, 2 * (NZ - 1) + 1 + 8)
 
-    def scatter(send, recv, ssem, rsem):
+    def scatter(pieces, to_cores):
         here = core * NZ + z
 
         def step(i, carry):
             d = step_of(NZ - 2 - i)
             r = lax.rem(z + d + NZ, NZ)
-            for to_core in (core, other):
-                remote(send.at[to_core * NZ + r], recv.at[here], ssem, rsem, at(d, 0, to_core)).start()
+            for to_core in to_cores:
+                for send, recv, ssem, rsem in pieces:
+                    remote(send.at[to_core * NZ + r], recv.at[here], ssem, rsem, at(d, 0, to_core)).start()
             return carry
 
         lax.fori_loop(0, NZ - 1, step, 0)
+
+    def within(send, recv, ssem, rsem):
+        here = core * NZ + z
         remote(send.at[other * NZ + z], recv.at[here], ssem, rsem, at(0, 0, other)).start()
         pltpu.make_async_copy(send.at[core * NZ + z], recv.at[here], rsem).start()
 
-    scatter(kv_send, kv_recv, kv_ss, kv_rs)
+    scatter([(kv_send, kv_recv, kv_ss, kv_rs)], (core, other))
+    within(kv_send, kv_recv, kv_ss, kv_rs)
 
     loads[2].wait()
     for j in range(CHUNKS):
         for h in range(2):
             first = (h * CHUNKS + j) * WIDE
-            q_send[j, h * NZ : (h + 1) * NZ] = permuted(q_in[:, first : first + WIDE])
+            moved = permuted(q_in[:, first : first + WIDE])
+            for w in range(2):
+                q_send[j, w, h * NZ : (h + 1) * NZ] = moved[:, :, w * 2 * D : (w + 1) * 2 * D]
 
     def send_queries(j, carry):
-        scatter(q_send.at[j], q_recv.at[j], q_ss.at[j], q_rs.at[j])
+        halves = [(q_send.at[j, w], q_recv.at[j, w], q_ss.at[j, w], q_rs.at[j, w]) for w in range(2)]
+        for piece in halves:
+            within(*piece)
+        for to_core in range(2):
+            for piece in halves:
+                scatter([piece], (to_core,))
         return carry
 
     lax.fori_loop(0, 4, send_queries, 0)
@@ -162,64 +174,66 @@
             remote(mine, band.at[j, pl.ds((2 - dc) * ROWS, ROWS)], halo_ss.at[j], halo_rs.at[j], at(0, dc, core)).start()
     drain(g_buf, g_rs)
 
-    def send_part(j, b):
-        to = part_recv.at[j, 2 - b // 2, core]
-        remote(part_send.at[j, b], to, part_ss.at[j], part_rs.at[j], at(0, b // 2 - 2, b % 2)).start()
+    def spread(j, i, first, second):
+        def send(b, device):
+            to = part_recv.at[j, i, 2 - b // 2, core]
+            remote(part_send.at[j, i, b], to, part_ss.at[j], part_rs.at[j], device).start()
+
+        for b in range(6):
+            total = first[b * D : (b + 1) * D] if b < 5 else second[4 * D :]
+            if 0 < b < 5:
+                total = total + second[(b - 1) * D : b * D]
+            part_send[j, i, b] = total.astype(BF16)
+            if b < 4:
+                send(b, at(0, b // 2 - 2, b % 2))
+        send(4 + other, at(0, 0, other))
+        pltpu.make_async_copy(part_send.at[j, i, 4 + core], part_recv.at[j, i, 0, core], part_rs.at[j]).start()
 
     def chunk(j):
         drain(band.at[j, pl.ds(0, 2 * ROWS)], halo_rs.at[j])
-        drain(q_recv.at[j], q_rs.at[j])
-        for t in range(2):
-            keys = band[j, t * D : t * D + BAND, :D]
-            values = band[j, t * D : t * D + BAND, D:]
-            q_rows = q_recv[j, t * NZ : (t + 1) * NZ].astype(F32).reshape(D, WIDE).astype(BF16)
-            g_rows = g_buf[t, :, columns(j * WIDE, WIDE)]
-            queries = jnp.concatenate([q_rows[:, a * D : (a + 1) * D] for a in range(GROUP)], axis=0)
-            grads = jnp.concatenate([g_rows[:, a * D : (a + 1) * D] for a in range(GROUP)], axis=0)
-            masked = jnp.concatenate([bias[t]] * GROUP, axis=1)
-            score = dot(keys, queries, 1, 1) * (SCALE * LOG2E) + masked
-            weight = jnp.exp2(score - jnp.max(score, axis=0, keepdims=True))
-            prob = weight * (1.0 / jnp.sum(weight, axis=0, keepdims=True))
-            prob_low = prob.astype(BF16)
-            grad_prob = dot(values, grads, 1, 1)
-            delta = jnp.sum(prob_low.astype(F32) * grad_prob, axis=0, keepdims=True)
-            grad_score = (prob * (grad_prob - delta) * SCALE).astype(BF16)
-            dk = dot(grad_score, queries, 1, 0)
-            dv = dot(prob_low, grads, 1, 0)
-            dq = dot(keys, grad_score, 0, 0)
-            for a in range(GROUP):
-                dq_stage[j, t, :, a * D : (a + 1) * D] = dq[:, a * D : (a + 1) * D].T.astype(BF16)
-            if t == 0:
-                acc[:, :D] = dk
-                acc[:, D:] = dv
-                part_send[j, 0, :, :D] = dk[:D].astype(BF16)
-                part_send[j, 0, :, D:] = dv[:D].astype(BF16)
-                send_part(j, 0)
-            else:
-                for b in range(1, 6):
-                    rows = slice(b * D, (b + 1) * D)
-                    if b < 5:
-                        k_sum, v_sum = acc[rows, :D], acc[rows, D:]
-                    k_new, v_new = dk[(b - 1) * D : b * D], dv[(b - 1) * D : b * D]
-                    k_sum = k_new if b == 5 else k_sum + k_new
-                    v_sum = v_new if b == 5 else v_sum + v_new
-                    part_send[j, b, :, :D] = k_sum.astype(BF16)
-                    part_send[j, b, :, D:] = v_sum.astype(BF16)
-        for b in range(1, 4):
-            send_part(j, b)
-        remote(part_send.at[j, 4 + other], part_recv.at[j, 0, core], part_ss.at[j], part_rs.at[j], at(0, 0, other)).start()
-        pltpu.make_async_copy(part_send.at[j, 4 + core], part_recv.at[j, 0, core], part_rs.at[j]).start()
+        keys = [band[j, t * D : t * D + BAND, :D] for t in range(2)]
+        values = [band[j, t * D : t * D + BAND, D:] for t in range(2)]
+        sums = {}
+        for w in range(2):
+            drain(q_recv.at[j, w], q_rs.at[j, w])
+            queries, grads, probs, lows, scores = ([] for _ in range(5))
+            for t in range(2):
+                q_rows = q_recv[j, w, t * NZ : (t + 1) * NZ].astype(F32).reshape(D, 2 * D).astype(BF16)
+                g_rows = g_buf[t, :, columns(j * WIDE + w * 2 * D, 2 * D)]
+                queries.append(jnp.concatenate([q_rows[:, :D], q_rows[:, D:]], axis=0))
+                grads.append(jnp.concatenate([g_rows[:, :D], g_rows[:, D:]], axis=0))
+                masked = jnp.concatenate([bias[t]] * 2, axis=1)
+                score = dot(keys[t], queries[t], 1, 1) * (SCALE * LOG2E) + masked
+                weight = jnp.exp2(score - jnp.max(score, axis=0, keepdims=True))
+                probs.append(weight * (1.0 / jnp.sum(weight, axis=0, keepdims=True)))
+                lows.append(probs[t].astype(BF16))
+                dv = dot(lows[t], grads[t], 1, 0)
+                sums[1, t] = dv if w == 0 else sums[1, t] + dv
+            if w == 1:
+                spread(j, 1, sums[1, 0], sums[1, 1])
+            for t in range(2):
+                grad_prob = dot(values[t], grads[t], 1, 1)
+                delta = jnp.sum(lows[t].astype(F32) * grad_prob, axis=0, keepdims=True)
+                scores.append((probs[t] * (grad_prob - delta) * SCALE).astype(BF16))
+                dk = dot(scores[t], queries[t], 1, 0)
+                sums[0, t] = dk if w == 0 else sums[0, t] + dk
+            if w == 1:
+                spread(j, 0, sums[0, 0], sums[0, 1])
+            for t in range(2):
+                dq = dot(keys[t], scores[t], 0, 0)
+                for a in range(2):
+                    first = (2 * w + a) * D
+                    dq_stage[j, t, :, first : first + D] = dq[:, a * D : (a + 1) * D].T.astype(BF16)
         to = dq_out.at[:, columns(core * half + j * WIDE, WIDE)]
         remote(dq_stage.at[j, other], to, dq_ss.at[j], dq_rs.at[j], at(0, 0, other)).start()
         pltpu.make_async_copy(dq_stage.at[j, core], to, dq_rs.at[j]).start()
 
     def fold(j):
         drain(part_recv.at[j], part_rs.at[j])
-        for h in range(2):
-            total = part_recv[j, 0, h].astype(F32) + part_recv[j, 1, h].astype(F32) + part_recv[j, 2, h].astype(F32)
-            total = total.astype(BF16)
-            dk_out[:, columns(h * WIDE + j * D, D)] = total[:, :D]
-            dv_out[:, columns(h * WIDE + j * D, D)] = total[:, D:]
+        for i, out in enumerate((dk_out, dv_out)):
+            for h in range(2):
+                near, mid, far = (part_recv[j, i, n, h].astype(F32) for n in range(3))
+                out[:, columns(h * WIDE + j * D, D)] = (near + mid + far).astype(BF16)
 
     def turn(j, carry):
         chunk(j)
@@ -237,8 +251,9 @@
     drain(g_buf.at[0], g_ss)
     drain(seg_band.at[pl.ds(0, 5)], seg_ss)
     for j in range(CHUNKS):
-        drain(q_send.at[j, pl.ds(0, 2 * NZ - 1)], q_ss.at[j])
-        drain(part_send.at[j, pl.ds(0, 5)], part_ss.at[j])
+        for w in range(2):
+            drain(q_send.at[j, w, pl.ds(0, 2 * NZ - 1)], q_ss.at[j, w])
+        drain(part_send.at[j, :, pl.ds(0, 5)], part_ss.at[j])
         drain(band.at[j, pl.ds(0, 2 * ROWS)], halo_ss.at[j])
         drain(dq_stage.at[j, 0], dq_ss.at[j])
         drain(dq_stage.at[j], dq_rs.at[j])
@@ -249,7 +264,7 @@
     vmem = pltpu.VMEM
     here = pl.BlockSpec(memory_space=vmem)
     apart = pl.BlockSpec(memory_space=pl.ANY)
-    return pl.pallas_call(
+    outs = pl.pallas_call(
         kernel,
         out_shape=(
             vmem((D, 2 * CHUNKS * WIDE), BF16),
@@ -263,24 +278,40 @@
             vmem((2, D, 2 * WIDE), BF16),
             vmem((2 * NZ, CAP, 2 * WIDE), BF16),
             vmem((2 * NZ, CAP, 2 * WIDE), BF16),
-            vmem((CHUNKS, 2 * NZ, CAP, WIDE), BF16),
-            vmem((CHUNKS, 2 * NZ, CAP, WIDE), BF16),
+            vmem((CHUNKS, 2, 2 * NZ, CAP, 2 * D), BF16),
+            vmem((CHUNKS, 2, 2 * NZ, CAP, 2 * D), BF16),
             vmem((2, D, CHUNKS * WIDE), BF16),
             vmem((CHUNKS, 3 * ROWS, 2 * D), BF16),
             vmem((8, D), jnp.int32),
             vmem((6, 8, D), jnp.int32),
             vmem((2, BAND, D), F32),
-            vmem((BAND, 2 * D), F32),
-            vmem((CHUNKS, 6, D, 2 * D), BF16),
-            vmem((CHUNKS, 3, 2, D, 2 * D), BF16),
+            vmem((CHUNKS, 2, 6, D, D), BF16),
+            vmem((CHUNKS, 2, 3, 2, D, D), BF16),
             vmem((CHUNKS, 2, D, WIDE), BF16),
-            dma((3,)), dma, dma, dma((CHUNKS,)), dma((CHUNKS,)), dma, dma, dma, dma, dma((CHUNKS,)), dma((CHUNKS,)),
+            dma((3,)), dma, dma, dma((CHUNKS, 2)), dma((CHUNKS, 2)), dma, dma, dma, dma, dma((CHUNKS,)), dma((CHUNKS,)),
             dma((CHUNKS,)), dma((CHUNKS,)), dma((CHUNKS,)), dma((CHUNKS,)),
         ],
         compiler_params=pltpu.CompilerParams(
             collective_id=0, has_side_effects=True, vmem_limit_bytes=56 << 20
         ),
     )(query_rows, source_key_rows, source_value_rows, grad_rows, routes.reshape(1, D), segments)
+    outs = [pltpu.with_memory_space_constraint(out, vmem) for out in outs]
+    return pl.pallas_call(
+        finish,
+        out_shape=tuple(jax.ShapeDtypeStruct(o.shape, o.dtype) for o in outs),
+        in_specs=[here] * 3,
+        out_specs=[apart] * 3,
+        scratch_shapes=[dma((3,))],
+    )(*outs)
+
+
+def finish(*refs):
+    sems = refs[-1]
+    copies = [pltpu.make_async_copy(refs[i], refs[3 + i], sems.at[i]) for i in range(3)]
+    for copy in copies:
+        copy.start()
+    for copy in copies:
+        copy.wait()
 
 
 def solution(mesh):

time: 99.9 us -> 95.9 us (0.960)
  local copies, waits for them, and re-layouts: 2.38 us -> 0 us
  Pallas kernels: 96.8 us -> 95.2 us
    pallas_call x1, Pallas kernels: 96.8 us -> 94 us  [body(): pl.pallas_call(kernel, out_shape=(vmem((D, 2 * CHUNKS * WIDE), BF16), vme...]
    unnamed x3 -> x0, local copies, waits for them, and re-layouts: 2.38 us -> none
    pallas_call x0 -> x1, Pallas kernels: none -> 1.16 us  [body(): pl.pallas_call(finish, out_shape=tuple((jax.ShapeDtypeStruct(o.shape, o.d...]
where the time goes in v3:
time: 95.9 us; the launch traced here: 95.8 us
  Pallas kernels  95.2 us (99%)
    pallas_call x1, Pallas kernels, body(): pl.pallas_call(kernel, out_shape=(vmem((D, 2 * CHUNKS * WIDE), BF16), vme...  94 us

profile of v3, /device:TPU:1, one launch (start us, length us, event | category | flops | bytes accessed | tf_op | source)
XLA Modules:
  0.0 95.8 jit_solution(6030060246314101891)
XLA Ops:
  0.6 94.0 %shard_map.85 = (bf16[128,4096]{1,0:T(8,128)(2,1)S(1)}, bf16[128,1024]{1,0:T(8,128)(2,1)S(1)}, bf16[128,1024]{1,0:T(8,128)(2,1)S(1)}) custom-call(bf16[128,4096]{1,0:T(8,128)(2,1)} %q_hbm.1, bf16[128,1024]{1,0:T(8,128)(2,1)} %k_hbm.1, bf16[128,1024]{1,0:T(8,128)(2,1)} %v_hbm.1, bf16[128,4096]{1,0:T(8,128)(2,1)} %g_hbm.1, s32[1,128]{1,0:T(1,128)} %bitcast.1, ...), custom_call_target="tpu_custom_call" | custom-call | tf_op jit(solution)/shard_map/pallas_call | solution.py:267
  94.6 1.2 %shard_map.86 = (bf16[128,4096]{1,0:T(8,128)(2,1)}, bf16[128,1024]{1,0:T(8,128)(2,1)}, bf16[128,1024]{1,0:T(8,128)(2,1)}) custom-call(bf16[128,4096]{1,0:T(8,128)(2,1)S(1)} %get-tuple-element.6.refs_0_, bf16[128,1024]{1,0:T(8,128)(2,1)S(1)} %get-tuple-element.7.refs_1_, bf16[128,1024]{1,0:T(8,128)(2,1)S(1)} %get-tuple-element.8.refs_2_), custom_call_target="tpu_custom_call" | custom-call | tf_op jit(solution)/shard_map/pallas_call | solution.py:299

commit v4 on v3

--- a/solution.py
+++ b/solution.py
@@ -177,7 +177,7 @@
     def spread(j, i, first, second):
         def send(b, device):
             to = part_recv.at[j, i, 2 - b // 2, core]
-            remote(part_send.at[j, i, b], to, part_ss.at[j], part_rs.at[j], device).start()
+            remote(part_send.at[j, i, b], to, part_ss.at[j], part_rs.at[j, i], device).start()
 
         for b in range(6):
             total = first[b * D : (b + 1) * D] if b < 5 else second[4 * D :]
@@ -187,7 +187,7 @@
             if b < 4:
                 send(b, at(0, b // 2 - 2, b % 2))
         send(4 + other, at(0, 0, other))
-        pltpu.make_async_copy(part_send.at[j, i, 4 + core], part_recv.at[j, i, 0, core], part_rs.at[j]).start()
+        pltpu.make_async_copy(part_send.at[j, i, 4 + core], part_recv.at[j, i, 0, core], part_rs.at[j, i]).start()
 
     def chunk(j):
         drain(band.at[j, pl.ds(0, 2 * ROWS)], halo_rs.at[j])
@@ -222,15 +222,14 @@
             for t in range(2):
                 dq = dot(keys[t], scores[t], 0, 0)
                 for a in range(2):
-                    first = (2 * w + a) * D
-                    dq_stage[j, t, :, first : first + D] = dq[:, a * D : (a + 1) * D].T.astype(BF16)
-        to = dq_out.at[:, columns(core * half + j * WIDE, WIDE)]
-        remote(dq_stage.at[j, other], to, dq_ss.at[j], dq_rs.at[j], at(0, 0, other)).start()
-        pltpu.make_async_copy(dq_stage.at[j, core], to, dq_rs.at[j]).start()
+                    dq_stage[j, w, t, :, a * D : (a + 1) * D] = dq[:, a * D : (a + 1) * D].T.astype(BF16)
+            to = dq_out.at[:, columns(core * half + (2 * j + w) * 2 * D, 2 * D)]
+            remote(dq_stage.at[j, w, other], to, dq_ss.at[j, w], dq_rs.at[j, w], at(0, 0, other)).start()
+            pltpu.make_async_copy(dq_stage.at[j, w, core], to, dq_rs.at[j, w]).start()
 
     def fold(j):
-        drain(part_recv.at[j], part_rs.at[j])
-        for i, out in enumerate((dk_out, dv_out)):
+        for i, out in ((1, dv_out), (0, dk_out)):
+            drain(part_recv.at[j, i], part_rs.at[j, i])
             for h in range(2):
                 near, mid, far = (part_recv[j, i, n, h].astype(F32) for n in range(3))
                 out[:, columns(h * WIDE + j * D, D)] = (near + mid + far).astype(BF16)
@@ -255,8 +254,9 @@
             drain(q_send.at[j, w, pl.ds(0, 2 * NZ - 1)], q_ss.at[j, w])
         drain(part_send.at[j, :, pl.ds(0, 5)], part_ss.at[j])
         drain(band.at[j, pl.ds(0, 2 * ROWS)], halo_ss.at[j])
-        drain(dq_stage.at[j, 0], dq_ss.at[j])
-        drain(dq_stage.at[j], dq_rs.at[j])
+        for w in range(2):
+            drain(dq_stage.at[j, w, 0], dq_ss.at[j, w])
+            drain(dq_stage.at[j, w], dq_rs.at[j, w])
 
 
 def body(query_rows, source_key_rows, source_value_rows, grad_rows, routes, segments):
@@ -287,9 +287,9 @@
             vmem((2, BAND, D), F32),
             vmem((CHUNKS, 2, 6, D, D), BF16),
             vmem((CHUNKS, 2, 3, 2, D, D), BF16),
-            vmem((CHUNKS, 2, D, WIDE), BF16),
+            vmem((CHUNKS, 2, 2, D, 2 * D), BF16),
             dma((3,)), dma, dma, dma((CHUNKS, 2)), dma((CHUNKS, 2)), dma, dma, dma, dma, dma((CHUNKS,)), dma((CHUNKS,)),
-            dma((CHUNKS,)), dma((CHUNKS,)), dma((CHUNKS,)), dma((CHUNKS,)),
+            dma((CHUNKS,)), dma((CHUNKS, 2)), dma((CHUNKS, 2)), dma((CHUNKS, 2)),
         ],
         compiler_params=pltpu.CompilerParams(
             collective_id=0, has_side_effects=True, vmem_limit_bytes=56 << 20

time: 95.9 us -> 96 us (level)
  no operation moved by 1% of the time
where the time goes in v4:
time: 96 us; the launch traced here: 95.9 us
  Pallas kernels  95.2 us (99%)
    pallas_call x1, Pallas kernels, body(): pl.pallas_call(kernel, out_shape=(vmem((D, 2 * CHUNKS * WIDE), BF16), vme...  94.1 us

profile of v4, /device:TPU:1, one launch (start us, length us, event | category | flops | bytes accessed | tf_op | source)
XLA Modules:
  0.0 95.9 jit_solution(13712266594864422673)
XLA Ops:
  0.6 94.1 %shard_map.85 = (bf16[128,4096]{1,0:T(8,128)(2,1)S(1)}, bf16[128,1024]{1,0:T(8,128)(2,1)S(1)}, bf16[128,1024]{1,0:T(8,128)(2,1)S(1)}) custom-call(bf16[128,4096]{1,0:T(8,128)(2,1)} %q_hbm.1, bf16[128,1024]{1,0:T(8,128)(2,1)} %k_hbm.1, bf16[128,1024]{1,0:T(8,128)(2,1)} %v_hbm.1, bf16[128,4096]{1,0:T(8,128)(2,1)} %g_hbm.1, s32[1,128]{1,0:T(1,128)} %bitcast.1, ...), custom_call_target="tpu_custom_call" | custom-call | tf_op jit(solution)/shard_map/pallas_call | solution.py:267
  94.7 1.2 %shard_map.86 = (bf16[128,4096]{1,0:T(8,128)(2,1)}, bf16[128,1024]{1,0:T(8,128)(2,1)}, bf16[128,1024]{1,0:T(8,128)(2,1)}) custom-call(bf16[128,4096]{1,0:T(8,128)(2,1)S(1)} %get-tuple-element.6.refs_0_, bf16[128,1024]{1,0:T(8,128)(2,1)S(1)} %get-tuple-element.7.refs_1_, bf16[128,1024]{1,0:T(8,128)(2,1)S(1)} %get-tuple-element.8.refs_2_), custom_call_target="tpu_custom_call" | custom-call | tf_op jit(solution)/shard_map/pallas_call | solution.py:299
